TPU v7x, 32 devices: a whole 2x2x4 slice. The times are simulated.
32 devices in a mesh: dp: 2 (over core), dom: 16 (over z, y, x).
Axes of the slice: x: 2, y: 2, z: 4, core: 2. Of those that a mesh axis runs over, the one named last changes fastest.
Arguments:
- features: bfloat16 [2, 6144, 512], P('dp', 'dom'), may hold values from -12 to 12
- tile_mask: int32 [2, 48, 18], P('dp', 'dom'), may hold values from 0 to 1, as said below
- cotangent: bfloat16 [2, 6144, 512], P('dp', 'dom'), may hold values from -6 to 6
- w_query: bfloat16 [512, 512], replicated, may hold values from -1 to 1
- w_key: bfloat16 [512, 512], replicated, may hold values from -1 to 1
- w_value: bfloat16 [512, 512], replicated, may hold values from -0.25 to 0.25
- w_out: bfloat16 [512, 512], replicated, may hold values from -0.25 to 0.25
Outputs:
- attended: bfloat16 [2, 6144, 512], P('dp', 'dom')
- grad_features: bfloat16 [2, 6144, 512], P('dp', 'dom')
- grad_query: float32 [512, 512], replicated
- grad_key: float32 [512, 512], replicated
- grad_value: float32 [512, 512], replicated
- grad_out: float32 [512, 512], replicated
Inputs may be any that keep to these rules, and one draw needn't show every extreme that they name: `tile_mask`: 0 or 1; the share of ones differs between tile groups, from about a quarter to all.
All inputs are finite; a program needn't handle non-finite values.
Results may differ from a plain program's by a relative error of at most 0.023.
Values may be sent and summed in bfloat16 or wider, within the bound.
No kernel may reach another device: no remote copies, remote signals or barrier semaphores. Data moves between devices by JAX's collectives and lax.ppermute only.
A program may use at most 128 MiB of HBM per device.

v0:
```python
import jax
import jax.numpy as jnp
from jax import lax
from jax.sharding import PartitionSpec as P

HEADS = 8
HEAD_DIM = 64
TILE = 128
TILE_DEV = 3
NB = 3
CANDT = 18


def with_halo(block, sides, width):
    for axis, dim in sides:
        count = lax.axis_size(axis)
        forward = [(i, i + 1) for i in range(count - 1)]
        forward.append((count - 1, 0))
        backward = [(target, source) for source, target in forward]
        low = lax.ppermute(
            lax.slice_in_dim(block, block.shape[dim] - width, None, axis=dim), axis, forward
        )
        high = lax.ppermute(lax.slice_in_dim(block, 0, width, axis=dim), axis, backward)
        block = jnp.concatenate([low, block, high], axis=dim)
    return block


def from_partner(value, axis, distance):
    mask = 2**distance
    pairs = [(source, source ^ mask) for source in range(lax.axis_size(axis))]
    return lax.ppermute(value, axis, pairs)


def candidate_blocks(block):
    block_rows = block.shape[0]
    near = with_halo(block, (("dom", 0),), block_rows)
    pieces = [block, near[:block_rows], near[2 * block_rows :]]
    levels = lax.axis_size("dom").bit_length() - 1
    for bit_step in range(NB):
        pieces.append(from_partner(block, "dom", levels - 1 - bit_step))
    return pieces


def returned_sum(grad_parts):
    block_rows = grad_parts.shape[1]
    outgoing = jnp.concatenate([grad_parts[1], grad_parts[2]], 0)
    returned = with_halo(outgoing, (("dom", 0),), block_rows)
    summed = grad_parts[0] + returned[:block_rows] + returned[3 * block_rows :]
    levels = lax.axis_size("dom").bit_length() - 1
    for bit_step in range(NB):
        summed = summed + from_partner(grad_parts[3 + bit_step], "dom", levels - 1 - bit_step)
    return summed


def joined(stacked_parts, width_all):
    return jnp.transpose(stacked_parts, (1, 0, 2)).reshape(stacked_parts.shape[1], width_all)


def per_device(features, tile_mask, cotangent, w_query, w_key, w_value, w_out):
    node_rows = features[0]
    block_rows = node_rows.shape[0]
    width_all = node_rows.shape[1]
    highest = lax.Precision.HIGHEST
    factor = HEAD_DIM ** (-0.5)
    w_both = jnp.concatenate([w_key, w_value], 1)
    q_rows = jnp.dot(node_rows, w_query, preferred_element_type=jnp.float32).astype(jnp.bfloat16)
    kv_rows = jnp.dot(node_rows, w_both, preferred_element_type=jnp.float32).astype(jnp.bfloat16)
    pieces = candidate_blocks(node_rows)
    remote = jnp.dot(
        jnp.concatenate(pieces[1:], 0), w_both, preferred_element_type=jnp.float32
    ).astype(jnp.bfloat16)
    cand_kv = jnp.concatenate([kv_rows, remote], 0)
    key_count = cand_kv.shape[0]
    keys_all = cand_kv[:, :width_all]
    values_all = cand_kv[:, width_all:]
    own_tile = jnp.arange(CANDT)[None, :] == jnp.arange(TILE_DEV)[:, None]
    live_tiles = (tile_mask[0] == 1) | own_tile
    masking = jnp.where(live_tiles, 0.0, -1e30).astype(jnp.float32)
    cot_rows = cotangent[0]
    grad_o = jnp.dot(cot_rows, w_out.T, preferred_element_type=jnp.float32).astype(jnp.bfloat16)
    pair_cols = 2 * HEAD_DIM

    def head_pair(pair_index):
        col_start = pair_index * pair_cols
        q_pair = lax.dynamic_slice_in_dim(q_rows, col_start, pair_cols, 1).reshape(
            block_rows, 2, HEAD_DIM
        )
        k_pair = lax.dynamic_slice_in_dim(keys_all, col_start, pair_cols, 1).reshape(
            key_count, 2, HEAD_DIM
        )
        v_pair = lax.dynamic_slice_in_dim(values_all, col_start, pair_cols, 1).reshape(
            key_count, 2, HEAD_DIM
        )
        g_pair = lax.dynamic_slice_in_dim(grad_o, col_start, pair_cols, 1).reshape(
            block_rows, 2, HEAD_DIM
        )
        scores = (
            jnp.einsum("rhd,chd->hrc", q_pair, k_pair, preferred_element_type=jnp.float32) * factor
        )
        scores = scores.reshape(2, TILE_DEV, TILE, CANDT, TILE) + masking[None, :, None, :, None]
        scores = scores.reshape(2, block_rows, key_count)
        row_max = jnp.max(scores, axis=2, keepdims=True)
        exp_vals = jnp.exp(scores - row_max)
        prob_f32 = exp_vals / jnp.sum(exp_vals, axis=2, keepdims=True)
        prob_bf = prob_f32.astype(jnp.bfloat16)
        out_pair = jnp.einsum(
            "hrc,chd->rhd", prob_bf, v_pair, preferred_element_type=jnp.float32
        ).astype(jnp.bfloat16)
        grad_prob = jnp.einsum("rhd,chd->hrc", g_pair, v_pair, preferred_element_type=jnp.float32)
        row_delta = jnp.einsum(
            "rhd,rhd->hr", g_pair.astype(jnp.float32), out_pair.astype(jnp.float32)
        )
        grad_score = (prob_f32 * (grad_prob - row_delta[:, :, None]) * factor).astype(jnp.bfloat16)
        gq_pair = jnp.einsum(
            "hrc,chd->rhd", grad_score, k_pair, preferred_element_type=jnp.float32
        ).reshape(block_rows, pair_cols)
        gk_pair = jnp.einsum(
            "hrc,rhd->chd", grad_score, q_pair, preferred_element_type=jnp.float32
        ).reshape(key_count, pair_cols)
        gv_pair = jnp.einsum(
            "hrc,rhd->chd", prob_bf, g_pair, preferred_element_type=jnp.float32
        ).reshape(key_count, pair_cols)
        return (out_pair.reshape(block_rows, pair_cols), gq_pair, gk_pair, gv_pair)

    stacked = lax.map(head_pair, jnp.arange(HEADS // 2, dtype=jnp.int32))
    out_rows = joined(stacked[0], width_all)
    grad_q = joined(stacked[1], width_all)
    grad_k = joined(stacked[2], width_all)
    grad_v = joined(stacked[3], width_all)
    attended = jnp.dot(out_rows, w_out, preferred_element_type=jnp.float32).astype(jnp.bfloat16)
    grad_parts = jnp.concatenate([grad_k, grad_v], 1).reshape(3 + NB, block_rows, 2 * width_all)
    w_both32 = w_both.astype(jnp.float32)
    rows_f32 = node_rows.astype(jnp.float32)
    contrib = jnp.einsum("scf,df->scd", grad_parts, w_both32, precision=highest)
    kv_dx = returned_sum(contrib)
    cand_rows = (
        jnp.concatenate(pieces, 0).reshape(3 + NB, block_rows, width_all).astype(jnp.float32)
    )
    g_both = jnp.einsum("scd,scf->df", cand_rows, grad_parts, precision=highest)
    grad_x = jnp.dot(grad_q, w_query.astype(jnp.float32).T, precision=highest) + kv_dx
    g_query = jnp.dot(rows_f32.T, grad_q, precision=highest)
    g_out = jnp.dot(out_rows.T, cot_rows, preferred_element_type=jnp.float32)
    g_query, g_key, g_value, g_out = lax.psum(
        (g_query, g_both[:, :width_all], g_both[:, width_all:], g_out), ("dp", "dom")
    )
    return (attended[None], grad_x.astype(jnp.bfloat16)[None], g_query, g_key, g_value, g_out)


def solution(mesh):
    in_specs = (
        P("dp", "dom", None),
        P("dp", "dom", None),
        P("dp", "dom", None),
        P(),
        P(),
        P(),
        P(),
    )
    out_specs = (P("dp", "dom", None), P("dp", "dom", None), P(), P(), P(), P())
    return jax.shard_map(
        per_device, mesh=mesh, in_specs=in_specs, out_specs=out_specs, check_vma=False
    )
```

profile of v0, /device:TPU:0, one launch (start us, length us, event | category | flops | bytes accessed | tf_op | source)
XLA Modules:
  0.0 415.0 jit_solution(7876235823481581899)
XLA Ops:
  7.2 3.1 collective-permute-start.3
  10.4 2.6 collective-permute-start.2
  13.0 2.1 collective-permute-start.1
  16.5 1.8 constant_dynamic-update-slice_fusion.18
  23.2 17.6 %collective-permute-done = bf16[384,512]{1,0:T(8,128)(2,1)} collective-permute-done((bf16[384,512]{1,0:T(8,128)(2,1)}, bf16[384,512]{1,0:T(8,128)(2,1)}, u32[]{:S(2)}, u32[]{:S(2)}) %collective-permute-start) | collective-permute-done | bytes 393248 | tf_op jit(solution)/shard_map/ppermute | solution.py:20
  40.8 1.8 constant_dynamic-update-slice_fusion.17
  42.7 1.8 constant_dynamic-update-slice_fusion.16
  44.5 1.8 constant_dynamic-update-slice_fusion.15
  46.3 1.8 constant_dynamic-update-slice_fusion.14
  48.1 1.8 constant_dynamic-update-slice_fusion.13
  49.9 2.2 convolution_convert_fusion.1
  52.1 3.8 pad_maximum_fusion
  55.9 110.8 %while.16 = (s32[]{:T(128)}, bf16[4,384,128]{1,2,0:T(8,128)(2,1)}, f32[4,384,128]{1,2,0:T(8,128)}, f32[4,2304,128]{1,2,0:T(8,128)}, f32[4,2304,128]{1,2,0:T(8,12...) while((s32[]{:T(128)}, bf16[4,384,128]{1,2,0:T(8,128)(2,1)}, ...), condition=%wide.region_3.4_spmd, body=%wide.region_0.3_spmd.sunk | while | flops 1378665984 | bytes 104414744 | solution.py:125
  60.7 2.5 copy.52
  63.2 7.1 %fusion.91 = (f32[2,384]{1,0:T(2,128)S(1)}, f32[2,384,2304]{2,1,0:T(8,128)}) fusion(f32[384,2304]{1,0:T(8,128)} %bitcast.170, bf16[384,2,64]{0,2,1:T(8,128)(2,1)S(1)} %bitcast.177, bf16[2304,2,64]{0,2,1:T(8,128)(2,1)S(1)} %bitcast.171), kind=kOutput, calls=%fused_computation.77.clone.1 | convolution fusion | flops 233572608 | bytes 11308032 | tf_op jit(solution)/shard_map/while/body/eval_jaxpr/sub | solution.py:103
  70.3 3.8 fusion.92
  77.1 1.6 multiply_convert_fusion.2
  82.0 1.7 constant_dynamic-update-slice_fusion.24
  88.4 2.5 copy.52
  90.9 7.1 %fusion.91 = (f32[2,384]{1,0:T(2,128)S(1)}, f32[2,384,2304]{2,1,0:T(8,128)}) fusion(f32[384,2304]{1,0:T(8,128)} %bitcast.170, bf16[384,2,64]{0,2,1:T(8,128)(2,1)S(1)} %bitcast.177, bf16[2304,2,64]{0,2,1:T(8,128)(2,1)S(1)} %bitcast.171), kind=kOutput, calls=%fused_computation.77.clone.1 | convolution fusion | flops 233572608 | bytes 11308032 | tf_op jit(solution)/shard_map/while/body/eval_jaxpr/sub | solution.py:103
  98.0 3.8 fusion.92
  104.9 1.6 multiply_convert_fusion.2
  109.8 1.6 constant_dynamic-update-slice_fusion.24
  116.2 2.5 copy.52
  118.7 7.1 %fusion.91 = (f32[2,384]{1,0:T(2,128)S(1)}, f32[2,384,2304]{2,1,0:T(8,128)}) fusion(f32[384,2304]{1,0:T(8,128)} %bitcast.170, bf16[384,2,64]{0,2,1:T(8,128)(2,1)S(1)} %bitcast.177, bf16[2304,2,64]{0,2,1:T(8,128)(2,1)S(1)} %bitcast.171), kind=kOutput, calls=%fused_computation.77.clone.1 | convolution fusion | flops 233572608 | bytes 11308032 | tf_op jit(solution)/shard_map/while/body/eval_jaxpr/sub | solution.py:103
  125.8 3.8 fusion.92
  132.6 1.6 multiply_convert_fusion.2
  143.8 2.5 copy.52
  146.3 7.1 %fusion.91 = (f32[2,384]{1,0:T(2,128)S(1)}, f32[2,384,2304]{2,1,0:T(8,128)}) fusion(f32[384,2304]{1,0:T(8,128)} %bitcast.170, bf16[384,2,64]{0,2,1:T(8,128)(2,1)S(1)} %bitcast.177, bf16[2304,2,64]{0,2,1:T(8,128)(2,1)S(1)} %bitcast.171), kind=kOutput, calls=%fused_computation.77.clone.1 | convolution fusion | flops 233572608 | bytes 11308032 | tf_op jit(solution)/shard_map/while/body/eval_jaxpr/sub | solution.py:103
  153.4 3.8 fusion.92
  160.3 1.6 multiply_convert_fusion.2
  166.7 6.4 %copy.25 = f32[2304,4,128]{2,1,0:T(4,128)} copy(f32[2304,4,128]{0,2,1:T(8,128)} %bitcast.185) | data formatting | bytes 9437184 | tf_op jit(solution)/shard_map/transpose | solution.py:56
  173.2 6.7 %concatenate.24 = f32[6,384,512]{2,1,0:T(8,128)} reshape(f32[2304,4,128]{2,1,0:T(4,128)} %copy.25) | data formatting | bytes 9437184 | tf_op jit(solution)/shard_map/concatenate | solution.py:131
  181.3 2.0 convolution_bitcast_fusion.1
  183.2 6.5 %copy.24 = f32[2304,4,128]{2,1,0:T(4,128)} copy(f32[2304,4,128]{0,2,1:T(8,128)} %bitcast.186) | data formatting | bytes 9437184 | tf_op jit(solution)/shard_map/transpose | solution.py:56
  189.7 6.6 %concatenate.23 = f32[6,384,512]{2,1,0:T(8,128)} reshape(f32[2304,4,128]{2,1,0:T(4,128)} %copy.24) | data formatting | bytes 9437184 | tf_op jit(solution)/shard_map/concatenate | solution.py:131
  196.3 3.0 constant_dynamic-update-slice_fusion.12
  202.0 7.7 %convolution_bitcast_fusion = f32[512,1024]{1,0:T(8,128)S(1)} fusion(bf16[6,384,512]{2,1,0:T(8,128)(2,1)S(1)} %bitcast.196, f32[6,384,1024]{2,1,0:T(8,128)S(1)} %constant_dynamic-update-slice_fusion.11), kind=kOutput, calls=%fused_computation.28 | convolution fusion | flops 14495514624 | bytes 13893632 | tf_op jit(solution)/shard_map/scd,scf->df/dot_general | solution.py:139
  211.2 10.5 %fusion.12 = f32[6,384,512]{2,1,0:T(8,128)S(1)} fusion(f32[6,384,1024]{2,1,0:T(8,128)} %copy-done.4, bf16[512,1024]{1,0:T(8,128)(2,1)S(1)} %copy-done.15), kind=kOutput, calls=%fused_computation.36 | convolution fusion | flops 14495514624 | bytes 15204352 | tf_op jit(solution)/shard_map/scf,df->scd/dot_general | solution.py:134
  224.4 4.2 %collective-permute-start.6 = (f32[384,512]{1,0:T(8,128)S(1)}, f32[384,512]{1,0:T(8,128)S(1)}, u32[]{:S(2)}, u32[]{:S(2)}) collective-permute-start(f32[384,512]{1,0:T(8,128)S(1)} %get-tuple-element.140), channel_id=1, source_target_pairs={{1,0},{2,1},{3,2},{4,3},{5,4},{6,5},{7,6},{8,7},{9,8},{10,9},{11,1... | collective-permute-start | bytes 2359304 | tf_op jit(solution)/shard_map/ppermute | solution.py:23
  229.8 24.6 %collective-permute-done.5 = f32[384,512]{1,0:T(8,128)S(1)} collective-permute-done((f32[384,512]{1,0:T(8,128)S(1)}, f32[384,512]{1,0:T(8,128)S(1)}, u32[]{:S(2)}, u32[]{:S(2)}) %collective-permute-start.5) | collective-permute-done | bytes 786464 | tf_op jit(solution)/shard_map/ppermute | solution.py:20
  254.4 7.0 %collective-permute-done.9 = f32[384,512]{1,0:T(8,128)S(1)} collective-permute-done((f32[384,512]{1,0:T(8,128)S(1)}, f32[384,512]{1,0:T(8,128)S(1)}, u32[]{:S(2)}, u32[]{:S(2)}) %collective-permute-start.9) | collective-permute-done | bytes 786464 | tf_op jit(solution)/shard_map/ppermute | solution.py:31
  261.4 9.6 %collective-permute-done.8 = f32[384,512]{1,0:T(8,128)S(1)} collective-permute-done((f32[384,512]{1,0:T(8,128)S(1)}, f32[384,512]{1,0:T(8,128)S(1)}, u32[]{:S(2)}, u32[]{:S(2)}) %collective-permute-start.8) | collective-permute-done | bytes 786464 | tf_op jit(solution)/shard_map/ppermute | solution.py:31
  271.4 16.0 %collective-permute-done.6 = f32[384,512]{1,0:T(8,128)S(1)} collective-permute-done((f32[384,512]{1,0:T(8,128)S(1)}, f32[384,512]{1,0:T(8,128)S(1)}, u32[]{:S(2)}, u32[]{:S(2)}) %collective-permute-start.6) | collective-permute-done | bytes 786464 | tf_op jit(solution)/shard_map/ppermute | solution.py:23
  287.4 2.4 fusion.21
  289.8 111.5 %all-reduce.3.cloned.1.call-done = (f32[512,512]{0,1:T(8,128)}, f32[512,512]{1,0:T(8,128)}, f32[512,512]{1,0:T(8,128)}, f32[512,512]{1,0:T(8,128)}) async-done(((f32[512,512]{0,1:T(8,128)}, f32[512,512]{1,0:T(8,128)}, f32[512,512]{1,0:T(8,128)}, f32[512,512]{1,0:T(8,128)}), (f32[512,512]{0,1:T(8,128)}, f32[512,512]{1,0:T(8,128)}, f32[512,512]{1,0:T(8,128)}, ...) | async-done | bytes 4194320 | tf_op jit(solution)/shard_map/psum | solution.py:143
  401.2 2.7 copy.27
  403.9 2.3 copy.89
  (157 shorter events, 62.2 us)
Async XLA Ops:
  7.2 15.5 %copy-start = (bf16[512,512]{1,0:T(8,128)(2,1)S(1)}, bf16[512,512]{1,0:T(8,128)(2,1)}, u32[]{:S(2)}) copy-start(bf16[512,512]{1,0:T(8,128)(2,1)} %param.15) | copy-start | bytes 1572868
  7.2 14.9 %copy-start.2 = (bf16[1,384,512]{2,1,0:T(8,128)(2,1)S(1)}, bf16[1,384,512]{2,1,0:T(8,128)(2,1)}, u32[]{:S(2)}) copy-start(bf16[1,384,512]{2,1,0:T(8,128)(2,1)} %param.9) | copy-start | bytes 1179652
  7.2 15.5 %copy-start.8 = (bf16[1,384,512]{2,1,0:T(8,128)(2,1)S(1)}, bf16[1,384,512]{2,1,0:T(8,128)(2,1)}, u32[]{:S(2)}) copy-start(bf16[1,384,512]{2,1,0:T(8,128)(2,1)} %param.11) | copy-start | bytes 1179652
  7.2 394.0 %all-reduce.3.cloned.1.call-start = ((), (), s32[]{:S(2)}) async-start(), calls=%async_computation | async-start | bytes 8388608 | tf_op jit(solution)/shard_map/psum | solution.py:143
  7.2 39.0 %collective-permute-start.3 = (bf16[384,512]{1,0:T(8,128)(2,1)}, bf16[384,512]{1,0:T(8,128)(2,1)}, u32[]{:S(2)}, u32[]{:S(2)}) collective-permute-start(bf16[384,512]{1,0:T(8,128)(2,1)} %bitcast.187), channel_id=1, source_target_pairs={{0,4},{1,5},{2,6},{3,7},{4,0},{5,1},{6,2},{7,3},{8,12},{9,13},{10,... | collective-permute-start | bytes 1179656 | tf_op jit(solution)/shard_map/ppermute | solution.py:31
  10.4 34.1 %collective-permute-start.2 = (bf16[384,512]{1,0:T(8,128)(2,1)}, bf16[384,512]{1,0:T(8,128)(2,1)}, u32[]{:S(2)}, u32[]{:S(2)}) collective-permute-start(bf16[384,512]{1,0:T(8,128)(2,1)} %bitcast.188), channel_id=1, source_target_pairs={{0,8},{1,9},{2,10},{3,11},{4,12},{5,13},{6,14},{7,15},{8,0},{9,1},... | collective-permute-start | bytes 1179656 | tf_op jit(solution)/shard_map/ppermute | solution.py:31
  13.0 29.7 %collective-permute-start.1 = (bf16[384,512]{1,0:T(8,128)(2,1)}, bf16[384,512]{1,0:T(8,128)(2,1)}, u32[]{:S(2)}, u32[]{:S(2)}) collective-permute-start(bf16[384,512]{1,0:T(8,128)(2,1)} %bitcast.189), channel_id=1, source_target_pairs={{1,0},{2,1},{3,2},{4,3},{5,4},{6,5},{7,6},{8,7},{9,8},{10,9},{11,1... | collective-permute-start | bytes 1179656 | tf_op jit(solution)/shard_map/ppermute | solution.py:23
  15.1 25.8 %collective-permute-start = (bf16[384,512]{1,0:T(8,128)(2,1)}, bf16[384,512]{1,0:T(8,128)(2,1)}, u32[]{:S(2)}, u32[]{:S(2)}) collective-permute-start(bf16[384,512]{1,0:T(8,128)(2,1)} %bitcast.190), channel_id=1, source_target_pairs={{0,1},{1,2},{2,3},{3,4},{4,5},{5,6},{6,7},{7,8},{8,9},{9,10},{10,1... | collective-permute-start | bytes 1179656 | tf_op jit(solution)/shard_map/ppermute | solution.py:20
  15.1 33.0 %collective-permute-start.4 = (bf16[384,512]{1,0:T(8,128)(2,1)}, bf16[384,512]{1,0:T(8,128)(2,1)}, u32[]{:S(2)}, u32[]{:S(2)}) collective-permute-start(bf16[384,512]{1,0:T(8,128)(2,1)} %bitcast.191), channel_id=1, source_target_pairs={{0,2},{1,3},{2,0},{3,1},{4,6},{5,7},{6,4},{7,5},{8,10},{9,11},{10,... | collective-permute-start | bytes 1179656 | tf_op jit(solution)/shard_map/ppermute | solution.py:31
  18.3 4.8 %copy-start.17 = (s32[1,3,18]{2,0,1:T(1,128)S(1)}, s32[1,3,18]{2,0,1:T(1,128)}, u32[]{:S(2)}) copy-start(s32[1,3,18]{2,0,1:T(1,128)} %param.10) | copy-start | bytes 652
  22.1 1.0 copy-start.13
  23.2 26.7 %copy-start.14 = (bf16[512,1024]{1,0:T(8,128)(2,1)S(1)}, bf16[512,1024]{1,0:T(8,128)(2,1)}, u32[]{:S(2)}) copy-start(bf16[512,1024]{1,0:T(8,128)(2,1)} %copy-done.13) | copy-start | bytes 3145732
  55.9 1.5 copy-start.6
  74.1 3.0 copy-start.1
  80.7 3.0 copy-start.7
  83.7 1.5 copy-start.6
  101.9 3.0 copy-start.1
  108.5 3.0 copy-start.7
  111.4 1.5 copy-start.6
  129.6 3.0 copy-start.1
  136.2 2.9 copy-start.7
  139.1 1.5 copy-start.6
  157.2 3.0 copy-start.1
  163.8 2.9 copy-start.7
  173.2 6.7 %copy-start.9 = (bf16[1,384,512]{2,1,0:T(8,128)(2,1)S(1)}, bf16[1,384,512]{2,1,0:T(8,128)(2,1)}, u32[]{:S(2)}) copy-start(bf16[1,384,512]{2,1,0:T(8,128)(2,1)} %param.11) | copy-start | bytes 1179652
  173.2 6.7 %copy-start.10 = (bf16[4,384,128]{1,2,0:T(8,128)(2,1)S(1)}, bf16[4,384,128]{1,2,0:T(8,128)(2,1)}, u32[]{:S(2)}) copy-start(bf16[4,384,128]{1,2,0:T(8,128)(2,1)} %get-tuple-element.66) | copy-start | bytes 1179652
  173.2 8.1 %copy-start.3 = (f32[4,384,128]{1,2,0:T(8,128)S(1)}, f32[4,384,128]{1,2,0:T(8,128)}, u32[]{:S(2)}) copy-start(f32[4,384,128]{1,2,0:T(8,128)} %get-tuple-element.67) | copy-start | bytes 2359300
  189.7 9.6 %slice-start = ((s8[4718592]{0:T(1024)(128)(4,1)}), s8[524288]{0:T(1024)(128)(4,1)S(1)}, s32[]{:S(2)}) async-start(s8[4718592]{0:T(1024)(128)(4,1)} %bitcast.182), calls=%async_computation.1 | async-start | bytes 1048576
  196.3 3.6 slice-start.1
  199.9 2.1 copy-start.16
  200.4 9.3 %copy-start.4 = (f32[6,384,1024]{2,1,0:T(8,128)}, f32[6,384,1024]{2,1,0:T(8,128)S(1)}, u32[]{:S(2)}) copy-start(f32[6,384,1024]{2,1,0:T(8,128)S(1)} %constant_dynamic-update-slice_fusion.11) | copy-start | bytes 28311556
  209.7 1.5 copy-start.15
  221.7 65.7 %copy-start.5 = (bf16[512,512]{1,0:T(8,128)(2,1)S(1)}, bf16[512,512]{1,0:T(8,128)(2,1)}, u32[]{:S(2)}) copy-start(bf16[512,512]{1,0:T(8,128)(2,1)} %param.12) | copy-start | bytes 1572868
  222.2 32.2 %collective-permute-start.5 = (f32[384,512]{1,0:T(8,128)S(1)}, f32[384,512]{1,0:T(8,128)S(1)}, u32[]{:S(2)}, u32[]{:S(2)}) collective-permute-start(f32[384,512]{1,0:T(8,128)S(1)} %get-tuple-element.136), channel_id=1, source_target_pairs={{0,1},{1,2},{2,3},{3,4},{4,5},{5,6},{6,7},{7,8},{8,9},{9,10},{10,1... | collective-permute-start | bytes 2359304 | tf_op jit(solution)/shard_map/ppermute | solution.py:20
  222.2 39.2 %collective-permute-start.9 = (f32[384,512]{1,0:T(8,128)S(1)}, f32[384,512]{1,0:T(8,128)S(1)}, u32[]{:S(2)}, u32[]{:S(2)}) collective-permute-start(f32[384,512]{1,0:T(8,128)S(1)} %get-tuple-element.137), channel_id=1, source_target_pairs={{0,2},{1,3},{2,0},{3,1},{4,6},{5,7},{6,4},{7,5},{8,10},{9,11},{10,... | collective-permute-start | bytes 2359304 | tf_op jit(solution)/shard_map/ppermute | solution.py:31
  222.3 48.7 %collective-permute-start.8 = (f32[384,512]{1,0:T(8,128)S(1)}, f32[384,512]{1,0:T(8,128)S(1)}, u32[]{:S(2)}, u32[]{:S(2)}) collective-permute-start(f32[384,512]{1,0:T(8,128)S(1)} %get-tuple-element.138), channel_id=1, source_target_pairs={{0,4},{1,5},{2,6},{3,7},{4,0},{5,1},{6,2},{7,3},{8,12},{9,13},{10,... | collective-permute-start | bytes 2359304 | tf_op jit(solution)/shard_map/ppermute | solution.py:31
  223.1 48.3 %collective-permute-start.7 = (f32[384,512]{1,0:T(8,128)S(1)}, f32[384,512]{1,0:T(8,128)S(1)}, u32[]{:S(2)}, u32[]{:S(2)}) collective-permute-start(f32[384,512]{1,0:T(8,128)S(1)} %get-tuple-element.139), channel_id=1, source_target_pairs={{0,8},{1,9},{2,10},{3,11},{4,12},{5,13},{6,14},{7,15},{8,0},{9,1},... | collective-permute-start | bytes 2359304 | tf_op jit(solution)/shard_map/ppermute | solution.py:31
  224.4 63.0 %collective-permute-start.6 = (f32[384,512]{1,0:T(8,128)S(1)}, f32[384,512]{1,0:T(8,128)S(1)}, u32[]{:S(2)}, u32[]{:S(2)}) collective-permute-start(f32[384,512]{1,0:T(8,128)S(1)} %get-tuple-element.140), channel_id=1, source_target_pairs={{1,0},{2,1},{3,2},{4,3},{5,4},{6,5},{7,6},{8,7},{9,8},{10,9},{11,1... | collective-permute-start | bytes 2359304 | tf_op jit(solution)/shard_map/ppermute | solution.py:23
  401.2 4.9 %copy-start.12 = (f32[512,512]{1,0:T(8,128)S(1)}, f32[512,512]{1,0:T(8,128)}, u32[]{:S(2)}) copy-start(f32[512,512]{1,0:T(8,128)} %get-tuple-element.283) | copy-start | bytes 3145732
  401.2 5.9 %copy-start.11 = (f32[512,512]{1,0:T(8,128)S(1)}, f32[512,512]{1,0:T(8,128)}, u32[]{:S(2)}) copy-start(f32[512,512]{1,0:T(8,128)} %get-tuple-element.284) | copy-start | bytes 3145732
Sparse Core Ops, SparseCore 0:
  211.3 189.8 all-reduce.2
where the time goes:
time: 417 us; the launch traced here: 415 us
  waiting for transfers between devices  187 us (45%)
  local copies, waits for them, and re-layouts  95.9 us (23%)
  matrix products  80.1 us (19%)
  other arithmetic  19.1 us (5%)
  starting transfers between devices  15.7 us (4%)
  between operations  14.3 us (3%)
    psum x1, waiting for transfers between devices, per_device(): lax.psum((g_query, g_both[:, :width_all], g_both[:, width_all:], g_out),...  111 us
    ppermute x2, waiting for transfers between devices, with_halo(): lax.ppermute(lax.slice_in_dim(block, block.shape[dim] - width, None, axis...  42.2 us
    sub x4, matrix products, head_pair(): exp_vals = jnp.exp(scores - row_max)  28.4 us
    unnamed x45, local copies, waits for them, and re-layouts  22.3 us
    ppermute x6, waiting for transfers between devices, from_partner(): return lax.ppermute(value, axis, pairs)  17 us
    ppermute x2, waiting for transfers between devices, with_halo(): lax.ppermute(lax.slice_in_dim(block, 0, width, axis=dim), axis, backward)  16 us
    convert_element_type x4, other arithmetic, head_pair(): prob_bf = prob_f32.astype(jnp.bfloat16)  15.3 us
    while x28, local copies, waits for them, and re-layouts  14.3 us
  transfers between devices with their start and end apart: 11, of which 7 were waited for; matrix products, arithmetic and copies ran while one was open for 7% of the time, Pallas kernels for 0%

commit v1 on v0

--- a/solution.py
+++ b/solution.py
@@ -141,7 +141,7 @@
     g_query = jnp.dot(rows_f32.T, grad_q, precision=highest)
     g_out = jnp.dot(out_rows.T, cot_rows, preferred_element_type=jnp.float32)
     g_query, g_key, g_value, g_out = lax.psum(
-        (g_query, g_both[:, :width_all], g_both[:, width_all:], g_out), ("dp", "dom")
+        lax.psum((g_query, g_both[:, :width_all], g_both[:, width_all:], g_out), "dom"), "dp"
     )
     return (attended[None], grad_x.astype(jnp.bfloat16)[None], g_query, g_key, g_value, g_out)
 

time: 417 us -> 460 us (1.10)
  waiting for transfers between devices: 187 us -> 227 us
    psum x1, waiting for transfers between devices: 111 us -> 166 us  [per_device(): lax.psum((g_query, g_both[:, :width_all], g_both[:, width_all:], g_out),...]
    ppermute x2, waiting for transfers between devices: 42.2 us -> 32.4 us  [with_halo(): lax.ppermute(lax.slice_in_dim(block, block.shape[dim] - width, None, axis...]
    ppermute x2, waiting for transfers between devices: 16 us -> 11.4 us  [with_halo(): lax.ppermute(lax.slice_in_dim(block, 0, width, axis=dim), axis, backward)]
  transfers between devices with their start and end apart: 11 -> 12, of which waited for: 7 -> 7; matrix products, arithmetic and copies ran while one was open for 7% -> 6% of each run, Pallas kernels for 0% -> 0%
where the time goes in v1:
time: 460 us; the launch traced here: 457 us
  waiting for transfers between devices  227 us (49%)
  local copies, waits for them, and re-layouts  95.9 us (21%)
  matrix products  80 us (17%)
  other arithmetic  19.1 us (4%)
  starting transfers between devices  17.6 us (4%)
  between operations  14.3 us (3%)
    psum x1, waiting for transfers between devices, per_device(): lax.psum((g_query, g_both[:, :width_all], g_both[:, width_all:], g_out),...  166 us
    ppermute x2, waiting for transfers between devices, with_halo(): lax.ppermute(lax.slice_in_dim(block, block.shape[dim] - width, None, axis...  32.4 us
    sub x4, matrix products, head_pair(): exp_vals = jnp.exp(scores - row_max)  28.3 us
    unnamed x45, local copies, waits for them, and re-layouts  22.3 us
    ppermute x6, waiting for transfers between devices, from_partner(): return lax.ppermute(value, axis, pairs)  17.4 us
    convert_element_type x4, other arithmetic, head_pair(): prob_bf = prob_f32.astype(jnp.bfloat16)  15.3 us
    while x28, local copies, waits for them, and re-layouts  14.3 us
    concatenate x3, local copies, waits for them, and re-layouts, per_device(): jnp.concatenate([grad_k, grad_v], 1)  13.7 us
  transfers between devices with their start and end apart: 12, of which 7 were waited for; matrix products, arithmetic and copies ran while one was open for 6% of the time, Pallas kernels for 0%

profile of v1, /device:TPU:0, one launch (start us, length us, event | category | flops | bytes accessed | tf_op | source)
XLA Modules:
  0.0 457.1 jit_solution(3954026942510519333)
XLA Ops:
  7.2 3.1 collective-permute-start.3
  10.4 2.6 collective-permute-start.2
  13.0 2.1 collective-permute-start.1
  16.5 1.8 constant_dynamic-update-slice_fusion.18
  23.2 17.6 %collective-permute-done = bf16[384,512]{1,0:T(8,128)(2,1)} collective-permute-done((bf16[384,512]{1,0:T(8,128)(2,1)}, bf16[384,512]{1,0:T(8,128)(2,1)}, u32[]{:S(2)}, u32[]{:S(2)}) %collective-permute-start) | collective-permute-done | bytes 393248 | tf_op jit(solution)/shard_map/ppermute | solution.py:20
  40.8 1.8 constant_dynamic-update-slice_fusion.17
  42.7 1.8 constant_dynamic-update-slice_fusion.16
  44.5 1.8 constant_dynamic-update-slice_fusion.15
  46.3 1.8 constant_dynamic-update-slice_fusion.14
  48.1 1.8 constant_dynamic-update-slice_fusion.13
  49.9 2.2 convolution_convert_fusion.1
  52.1 3.8 pad_maximum_fusion
  56.0 110.7 %while.16 = (s32[]{:T(128)}, bf16[4,384,128]{1,2,0:T(8,128)(2,1)}, f32[4,384,128]{1,2,0:T(8,128)}, f32[4,2304,128]{1,2,0:T(8,128)}, f32[4,2304,128]{1,2,0:T(8,12...) while((s32[]{:T(128)}, bf16[4,384,128]{1,2,0:T(8,128)(2,1)}, ...), condition=%wide.region_3.4_spmd, body=%wide.region_0.3_spmd.sunk | while | flops 1378665984 | bytes 104414744 | solution.py:125
  60.7 2.5 copy.52
  63.2 7.1 %fusion.91 = (f32[2,384]{1,0:T(2,128)S(1)}, f32[2,384,2304]{2,1,0:T(8,128)}) fusion(f32[384,2304]{1,0:T(8,128)} %bitcast.170, bf16[384,2,64]{0,2,1:T(8,128)(2,1)S(1)} %bitcast.177, bf16[2304,2,64]{0,2,1:T(8,128)(2,1)S(1)} %bitcast.171), kind=kOutput, calls=%fused_computation.77.clone.1 | convolution fusion | flops 233572608 | bytes 11308032 | tf_op jit(solution)/shard_map/while/body/eval_jaxpr/sub | solution.py:103
  70.3 3.8 fusion.92
  77.1 1.6 multiply_convert_fusion.2
  82.0 1.7 constant_dynamic-update-slice_fusion.24
  88.4 2.5 copy.52
  90.9 7.1 %fusion.91 = (f32[2,384]{1,0:T(2,128)S(1)}, f32[2,384,2304]{2,1,0:T(8,128)}) fusion(f32[384,2304]{1,0:T(8,128)} %bitcast.170, bf16[384,2,64]{0,2,1:T(8,128)(2,1)S(1)} %bitcast.177, bf16[2304,2,64]{0,2,1:T(8,128)(2,1)S(1)} %bitcast.171), kind=kOutput, calls=%fused_computation.77.clone.1 | convolution fusion | flops 233572608 | bytes 11308032 | tf_op jit(solution)/shard_map/while/body/eval_jaxpr/sub | solution.py:103
  98.0 3.8 fusion.92
  104.9 1.6 multiply_convert_fusion.2
  109.8 1.6 constant_dynamic-update-slice_fusion.24
  116.1 2.5 copy.52
  118.6 7.1 %fusion.91 = (f32[2,384]{1,0:T(2,128)S(1)}, f32[2,384,2304]{2,1,0:T(8,128)}) fusion(f32[384,2304]{1,0:T(8,128)} %bitcast.170, bf16[384,2,64]{0,2,1:T(8,128)(2,1)S(1)} %bitcast.177, bf16[2304,2,64]{0,2,1:T(8,128)(2,1)S(1)} %bitcast.171), kind=kOutput, calls=%fused_computation.77.clone.1 | convolution fusion | flops 233572608 | bytes 11308032 | tf_op jit(solution)/shard_map/while/body/eval_jaxpr/sub | solution.py:103
  125.7 3.8 fusion.92
  132.5 1.6 multiply_convert_fusion.2
  143.8 2.5 copy.52
  146.3 7.1 %fusion.91 = (f32[2,384]{1,0:T(2,128)S(1)}, f32[2,384,2304]{2,1,0:T(8,128)}) fusion(f32[384,2304]{1,0:T(8,128)} %bitcast.170, bf16[384,2,64]{0,2,1:T(8,128)(2,1)S(1)} %bitcast.177, bf16[2304,2,64]{0,2,1:T(8,128)(2,1)S(1)} %bitcast.171), kind=kOutput, calls=%fused_computation.77.clone.1 | convolution fusion | flops 233572608 | bytes 11308032 | tf_op jit(solution)/shard_map/while/body/eval_jaxpr/sub | solution.py:103
  153.4 3.8 fusion.92
  160.2 1.6 multiply_convert_fusion.2
  166.7 6.5 %copy.25 = f32[2304,4,128]{2,1,0:T(4,128)} copy(f32[2304,4,128]{0,2,1:T(8,128)} %bitcast.185) | data formatting | bytes 9437184 | tf_op jit(solution)/shard_map/transpose | solution.py:56
  173.2 6.6 %concatenate.24 = f32[6,384,512]{2,1,0:T(8,128)} reshape(f32[2304,4,128]{2,1,0:T(4,128)} %copy.25) | data formatting | bytes 9437184 | tf_op jit(solution)/shard_map/concatenate | solution.py:131
  181.2 2.0 convolution_bitcast_fusion.1
  183.2 6.4 %copy.24 = f32[2304,4,128]{2,1,0:T(4,128)} copy(f32[2304,4,128]{0,2,1:T(8,128)} %bitcast.186) | data formatting | bytes 9437184 | tf_op jit(solution)/shard_map/transpose | solution.py:56
  189.6 6.6 %concatenate.23 = f32[6,384,512]{2,1,0:T(8,128)} reshape(f32[2304,4,128]{2,1,0:T(4,128)} %copy.24) | data formatting | bytes 9437184 | tf_op jit(solution)/shard_map/concatenate | solution.py:131
  196.2 3.0 constant_dynamic-update-slice_fusion.12
  201.9 7.7 %convolution_bitcast_fusion = f32[512,1024]{1,0:T(8,128)S(1)} fusion(bf16[6,384,512]{2,1,0:T(8,128)(2,1)S(1)} %bitcast.196, f32[6,384,1024]{2,1,0:T(8,128)S(1)} %constant_dynamic-update-slice_fusion.11), kind=kOutput, calls=%fused_computation.28 | convolution fusion | flops 14495514624 | bytes 13893632 | tf_op jit(solution)/shard_map/scd,scf->df/dot_general | solution.py:139
  211.2 165.9 %all-reduce.5.cloned.1.call-done = (f32[512,512]{0,1:T(8,128)}, f32[512,512]{1,0:T(8,128)}, f32[512,512]{1,0:T(8,128)}, f32[512,512]{1,0:T(8,128)}) async-done(((f32[512,512]{0,1:T(8,128)}, f32[512,512]{1,0:T(8,128)}, f32[512,512]{1,0:T(8,128)}, f32[512,512]{1,0:T(8,128)}), (f32[512,512]{0,1:T(8,128)}, f32[512,512]{1,0:T(8,128)}, f32[512,512]{1,0:T(8,128)}, ...) | async-done | bytes 4194320 | tf_op jit(solution)/shard_map/psum | solution.py:144
  377.2 10.5 %fusion.12 = f32[6,384,512]{2,1,0:T(8,128)S(1)} fusion(f32[6,384,1024]{2,1,0:T(8,128)} %copy-done.4, bf16[512,1024]{1,0:T(8,128)(2,1)S(1)} %copy-done.15), kind=kOutput, calls=%fused_computation.36 | convolution fusion | flops 14495514624 | bytes 15204352 | tf_op jit(solution)/shard_map/scf,df->scd/dot_general | solution.py:134
  393.0 3.3 collective-permute-start.6
  397.5 14.8 %collective-permute-done.5 = f32[384,512]{1,0:T(8,128)S(1)} collective-permute-done((f32[384,512]{1,0:T(8,128)S(1)}, f32[384,512]{1,0:T(8,128)S(1)}, u32[]{:S(2)}, u32[]{:S(2)}) %collective-permute-start.5) | collective-permute-done | bytes 786464 | tf_op jit(solution)/shard_map/ppermute | solution.py:20
  412.3 12.8 %collective-permute-done.9 = f32[384,512]{1,0:T(8,128)S(1)} collective-permute-done((f32[384,512]{1,0:T(8,128)S(1)}, f32[384,512]{1,0:T(8,128)S(1)}, u32[]{:S(2)}, u32[]{:S(2)}) %collective-permute-start.9) | collective-permute-done | bytes 786464 | tf_op jit(solution)/shard_map/ppermute | solution.py:31
  426.4 3.2 collective-permute-done.7
  429.7 11.4 %collective-permute-done.6 = f32[384,512]{1,0:T(8,128)S(1)} collective-permute-done((f32[384,512]{1,0:T(8,128)S(1)}, f32[384,512]{1,0:T(8,128)S(1)}, u32[]{:S(2)}, u32[]{:S(2)}) %collective-permute-start.6) | collective-permute-done | bytes 786464 | tf_op jit(solution)/shard_map/ppermute | solution.py:23
  441.0 2.4 fusion.21
  443.4 2.7 copy.27
  446.1 2.3 copy.93
  (160 shorter events, 65.9 us)
Async XLA Ops:
  7.2 15.5 %copy-start = (bf16[512,512]{1,0:T(8,128)(2,1)S(1)}, bf16[512,512]{1,0:T(8,128)(2,1)}, u32[]{:S(2)}) copy-start(bf16[512,512]{1,0:T(8,128)(2,1)} %param.15) | copy-start | bytes 1572868
  7.2 14.9 %copy-start.2 = (bf16[1,384,512]{2,1,0:T(8,128)(2,1)S(1)}, bf16[1,384,512]{2,1,0:T(8,128)(2,1)}, u32[]{:S(2)}) copy-start(bf16[1,384,512]{2,1,0:T(8,128)(2,1)} %param.9) | copy-start | bytes 1179652
  7.2 15.5 %copy-start.8 = (bf16[1,384,512]{2,1,0:T(8,128)(2,1)S(1)}, bf16[1,384,512]{2,1,0:T(8,128)(2,1)}, u32[]{:S(2)}) copy-start(bf16[1,384,512]{2,1,0:T(8,128)(2,1)} %param.11) | copy-start | bytes 1179652
  7.2 369.9 %all-reduce.5.cloned.1.call-start = ((), (), s32[]{:S(2)}) async-start(), calls=%async_computation | async-start | bytes 8388608 | tf_op jit(solution)/shard_map/psum | solution.py:144
  7.2 39.0 %collective-permute-start.3 = (bf16[384,512]{1,0:T(8,128)(2,1)}, bf16[384,512]{1,0:T(8,128)(2,1)}, u32[]{:S(2)}, u32[]{:S(2)}) collective-permute-start(bf16[384,512]{1,0:T(8,128)(2,1)} %bitcast.187), channel_id=1, source_target_pairs={{0,4},{1,5},{2,6},{3,7},{4,0},{5,1},{6,2},{7,3},{8,12},{9,13},{10,... | collective-permute-start | bytes 1179656 | tf_op jit(solution)/shard_map/ppermute | solution.py:31
  10.4 34.1 %collective-permute-start.2 = (bf16[384,512]{1,0:T(8,128)(2,1)}, bf16[384,512]{1,0:T(8,128)(2,1)}, u32[]{:S(2)}, u32[]{:S(2)}) collective-permute-start(bf16[384,512]{1,0:T(8,128)(2,1)} %bitcast.188), channel_id=1, source_target_pairs={{0,8},{1,9},{2,10},{3,11},{4,12},{5,13},{6,14},{7,15},{8,0},{9,1},... | collective-permute-start | bytes 1179656 | tf_op jit(solution)/shard_map/ppermute | solution.py:31
  13.0 29.7 %collective-permute-start.1 = (bf16[384,512]{1,0:T(8,128)(2,1)}, bf16[384,512]{1,0:T(8,128)(2,1)}, u32[]{:S(2)}, u32[]{:S(2)}) collective-permute-start(bf16[384,512]{1,0:T(8,128)(2,1)} %bitcast.189), channel_id=1, source_target_pairs={{1,0},{2,1},{3,2},{4,3},{5,4},{6,5},{7,6},{8,7},{9,8},{10,9},{11,1... | collective-permute-start | bytes 1179656 | tf_op jit(solution)/shard_map/ppermute | solution.py:23
  15.1 25.8 %collective-permute-start = (bf16[384,512]{1,0:T(8,128)(2,1)}, bf16[384,512]{1,0:T(8,128)(2,1)}, u32[]{:S(2)}, u32[]{:S(2)}) collective-permute-start(bf16[384,512]{1,0:T(8,128)(2,1)} %bitcast.190), channel_id=1, source_target_pairs={{0,1},{1,2},{2,3},{3,4},{4,5},{5,6},{6,7},{7,8},{8,9},{9,10},{10,1... | collective-permute-start | bytes 1179656 | tf_op jit(solution)/shard_map/ppermute | solution.py:20
  15.1 33.0 %collective-permute-start.4 = (bf16[384,512]{1,0:T(8,128)(2,1)}, bf16[384,512]{1,0:T(8,128)(2,1)}, u32[]{:S(2)}, u32[]{:S(2)}) collective-permute-start(bf16[384,512]{1,0:T(8,128)(2,1)} %bitcast.191), channel_id=1, source_target_pairs={{0,2},{1,3},{2,0},{3,1},{4,6},{5,7},{6,4},{7,5},{8,10},{9,11},{10,... | collective-permute-start | bytes 1179656 | tf_op jit(solution)/shard_map/ppermute | solution.py:31
  18.3 4.8 %copy-start.17 = (s32[1,3,18]{2,0,1:T(1,128)S(1)}, s32[1,3,18]{2,0,1:T(1,128)}, u32[]{:S(2)}) copy-start(s32[1,3,18]{2,0,1:T(1,128)} %param.10) | copy-start | bytes 652
  22.1 1.0 copy-start.13
  23.2 26.7 %copy-start.14 = (bf16[512,1024]{1,0:T(8,128)(2,1)S(1)}, bf16[512,1024]{1,0:T(8,128)(2,1)}, u32[]{:S(2)}) copy-start(bf16[512,1024]{1,0:T(8,128)(2,1)} %copy-done.13) | copy-start | bytes 3145732
  56.0 1.5 copy-start.6
  74.1 3.0 copy-start.1
  80.7 3.0 copy-start.7
  83.7 1.5 copy-start.6
  101.8 3.0 copy-start.1
  108.4 3.0 copy-start.7
  111.4 1.5 copy-start.6
  129.5 3.0 copy-start.1
  136.1 2.9 copy-start.7
  139.1 1.5 copy-start.6
  157.2 3.0 copy-start.1
  163.8 2.9 copy-start.7
  173.1 6.7 %copy-start.9 = (bf16[1,384,512]{2,1,0:T(8,128)(2,1)S(1)}, bf16[1,384,512]{2,1,0:T(8,128)(2,1)}, u32[]{:S(2)}) copy-start(bf16[1,384,512]{2,1,0:T(8,128)(2,1)} %param.11) | copy-start | bytes 1179652
  173.1 6.7 %copy-start.10 = (bf16[4,384,128]{1,2,0:T(8,128)(2,1)S(1)}, bf16[4,384,128]{1,2,0:T(8,128)(2,1)}, u32[]{:S(2)}) copy-start(bf16[4,384,128]{1,2,0:T(8,128)(2,1)} %get-tuple-element.66) | copy-start | bytes 1179652
  173.1 8.1 %copy-start.3 = (f32[4,384,128]{1,2,0:T(8,128)S(1)}, f32[4,384,128]{1,2,0:T(8,128)}, u32[]{:S(2)}) copy-start(f32[4,384,128]{1,2,0:T(8,128)} %get-tuple-element.67) | copy-start | bytes 2359300
  189.6 9.6 %slice-start = ((s8[4718592]{0:T(1024)(128)(4,1)}), s8[524288]{0:T(1024)(128)(4,1)S(1)}, s32[]{:S(2)}) async-start(s8[4718592]{0:T(1024)(128)(4,1)} %bitcast.182), calls=%async_computation.2 | async-start | bytes 1048576
  196.2 3.6 slice-start.1
  199.8 2.1 copy-start.16
  200.3 9.3 %copy-start.4 = (f32[6,384,1024]{2,1,0:T(8,128)}, f32[6,384,1024]{2,1,0:T(8,128)S(1)}, u32[]{:S(2)}) copy-start(f32[6,384,1024]{2,1,0:T(8,128)S(1)} %constant_dynamic-update-slice_fusion.11) | copy-start | bytes 28311556
  211.1 166.0 %copy-start.15 = (bf16[512,1024]{1,0:T(8,128)(2,1)S(1)}, bf16[512,1024]{1,0:T(8,128)(2,1)}, u32[]{:S(2)}) copy-start(bf16[512,1024]{1,0:T(8,128)(2,1)} %copy-done.13) | copy-start | bytes 3145732
  211.2 232.2 %all-reduce.7.cloned.1.call-start = ((), (), s32[]{:S(2)}) async-start(), calls=%async_computation.1 | async-start | bytes 8388608 | tf_op jit(solution)/shard_map/psum | solution.py:143
  387.7 53.4 %copy-start.5 = (bf16[512,512]{1,0:T(8,128)(2,1)S(1)}, bf16[512,512]{1,0:T(8,128)(2,1)}, u32[]{:S(2)}) copy-start(bf16[512,512]{1,0:T(8,128)(2,1)} %param.12) | copy-start | bytes 1572868
  388.1 24.2 %collective-permute-start.5 = (f32[384,512]{1,0:T(8,128)S(1)}, f32[384,512]{1,0:T(8,128)S(1)}, u32[]{:S(2)}, u32[]{:S(2)}) collective-permute-start(f32[384,512]{1,0:T(8,128)S(1)} %get-tuple-element.140), channel_id=1, source_target_pairs={{0,1},{1,2},{2,3},{3,4},{4,5},{5,6},{6,7},{7,8},{8,9},{9,10},{10,1... | collective-permute-start | bytes 2359304 | tf_op jit(solution)/shard_map/ppermute | solution.py:20
  389.6 35.5 %collective-permute-start.9 = (f32[384,512]{1,0:T(8,128)S(1)}, f32[384,512]{1,0:T(8,128)S(1)}, u32[]{:S(2)}, u32[]{:S(2)}) collective-permute-start(f32[384,512]{1,0:T(8,128)S(1)} %get-tuple-element.141), channel_id=1, source_target_pairs={{0,2},{1,3},{2,0},{3,1},{4,6},{5,7},{6,4},{7,5},{8,10},{9,11},{10,... | collective-permute-start | bytes 2359304 | tf_op jit(solution)/shard_map/ppermute | solution.py:31
  391.1 35.3 %collective-permute-start.8 = (f32[384,512]{1,0:T(8,128)S(1)}, f32[384,512]{1,0:T(8,128)S(1)}, u32[]{:S(2)}, u32[]{:S(2)}) collective-permute-start(f32[384,512]{1,0:T(8,128)S(1)} %get-tuple-element.142), channel_id=1, source_target_pairs={{0,4},{1,5},{2,6},{3,7},{4,0},{5,1},{6,2},{7,3},{8,12},{9,13},{10,... | collective-permute-start | bytes 2359304 | tf_op jit(solution)/shard_map/ppermute | solution.py:31
  391.5 38.2 %collective-permute-start.7 = (f32[384,512]{1,0:T(8,128)S(1)}, f32[384,512]{1,0:T(8,128)S(1)}, u32[]{:S(2)}, u32[]{:S(2)}) collective-permute-start(f32[384,512]{1,0:T(8,128)S(1)} %get-tuple-element.143), channel_id=1, source_target_pairs={{0,8},{1,9},{2,10},{3,11},{4,12},{5,13},{6,14},{7,15},{8,0},{9,1},... | collective-permute-start | bytes 2359304 | tf_op jit(solution)/shard_map/ppermute | solution.py:31
  393.0 48.0 %collective-permute-start.6 = (f32[384,512]{1,0:T(8,128)S(1)}, f32[384,512]{1,0:T(8,128)S(1)}, u32[]{:S(2)}, u32[]{:S(2)}) collective-permute-start(f32[384,512]{1,0:T(8,128)S(1)} %get-tuple-element.144), channel_id=1, source_target_pairs={{1,0},{2,1},{3,2},{4,3},{5,4},{6,5},{7,6},{8,7},{9,8},{10,9},{11,1... | collective-permute-start | bytes 2359304 | tf_op jit(solution)/shard_map/ppermute | solution.py:23
  443.4 4.9 %copy-start.12 = (f32[512,512]{1,0:T(8,128)S(1)}, f32[512,512]{1,0:T(8,128)}, u32[]{:S(2)}) copy-start(f32[512,512]{1,0:T(8,128)} %get-tuple-element.287) | copy-start | bytes 3145732
  443.4 5.9 %copy-start.11 = (f32[512,512]{1,0:T(8,128)S(1)}, f32[512,512]{1,0:T(8,128)}, u32[]{:S(2)}) copy-start(f32[512,512]{1,0:T(8,128)} %get-tuple-element.288) | copy-start | bytes 3145732
Sparse Core Ops, SparseCore 0:
  211.3 165.8 all-reduce.4
  379.9 27.5 all-reduce.6
